TPU v7x, 128 devices: a whole 4x4x4 slice. The times are simulated.
128 devices in a mesh: grp: 8 (over z_hi, x), aux: 16 (over y, z_lo, core).
Axes of the slice: x: 4, y: 4, z: 4 (z_hi: 2, z_lo: 2; z = z_hi * 2 + z_lo), core: 2. Of those that a mesh axis runs over, the one named last changes fastest.
Arguments:
- integrals: float32 [1536, 256, 384], P('aux', 'grp'), may hold values from -0.8 to 0.8
- occ_energy: float32 [256], replicated, may hold values from -2 to -0.3
- vir_energy: float32 [384], replicated, may hold values from 0.2 to 3
- orbital_order: int32 [256], replicated, may hold values from 0 to 255, each once
- owners: int32 [1, 8], replicated, may hold values from 0 to 15, as said below
Outputs:
- density: float32 [1536, 256, 384], P('aux', 'grp')
Inputs may be any that keep to these rules, and one draw needn't show every extreme that they name: `orbital_order`: a permutation of the table's entries. owners[s, g] names one of the 16 blocks of the group before g.
All inputs are finite; a program needn't handle non-finite values.
Results may differ from a plain program's by a relative error of at most 0.00011.
Values sent between devices are 32-bit elements; how exact they have to be, the bound alone decides.
A program may use at most 64 MiB of HBM per device.

v0:
```python
import jax
import jax.numpy as jnp
from jax import lax
from jax.sharding import PartitionSpec as P

level_shift = 0.5


def from_behind(block, axis, distance):
    devices = range(lax.axis_size(axis))
    route = [((i - distance) % len(devices), i) for i in devices]
    return lax.ppermute(block, axis, route)


def from_root(value, axis, source):
    kept = jnp.where(lax.axis_index(axis) == source, value, 0).astype(value.dtype)
    return lax.psum(kept, axis)


def body(integrals, occ_energy, vir_energy, orbital_order, owners):
    highest = lax.Precision.HIGHEST
    n_groups = lax.axis_size("grp")
    grp_index = lax.axis_index("grp")
    aux_index = lax.axis_index("aux")
    group_occ = integrals.shape[1]
    n_vir = integrals.shape[2]
    n_occ = occ_energy.shape[0]
    owned = lax.all_to_all(integrals, "aux", split_axis=1, concat_axis=0, tiled=True)
    n_auxfun = owned.shape[0]
    occ_block = owned.shape[1]
    mine_flat = owned.reshape(n_auxfun, occ_block * n_vir)
    onehot = (orbital_order[:, None] == jnp.arange(n_occ, dtype=jnp.int32)[None, :]).astype(
        jnp.float32
    )
    levels = jnp.dot(onehot, occ_energy, precision=highest, preferred_element_type=jnp.float32)
    mine_start = grp_index * group_occ + aux_index * occ_block
    mine_levels = lax.dynamic_slice_in_dim(levels, mine_start, occ_block, 0)
    source_group = (grp_index + n_groups - 1) % n_groups
    my_owners = lax.dynamic_index_in_dim(owners, grp_index, 1, keepdims=False)
    neighbour = from_behind(owned, "grp", 1)
    vir_pair = vir_energy[None, :, None, None] + vir_energy[None, None, None, :]
    owner_now = my_owners[0]
    j_block = from_root(neighbour, "aux", owner_now)
    j_flat = j_block.reshape(n_auxfun, occ_block * n_vir)
    j_levels = lax.dynamic_slice_in_dim(
        levels, source_group * group_occ + owner_now * occ_block, occ_block, 0
    )
    pair_flat = lax.dot_general(
        mine_flat,
        j_flat,
        (((0,), (0,)), ((), ())),
        precision=highest,
        preferred_element_type=jnp.float32,
    )
    pair_ints = pair_flat.reshape(occ_block, n_vir, occ_block, n_vir)
    swapped = jnp.transpose(pair_ints, (0, 3, 2, 1))
    gaps = vir_pair - mine_levels[:, None, None, None] - j_levels[None, None, :, None] + level_shift
    amplitude = ((2.0 * pair_ints - swapped) / gaps).reshape(occ_block * n_vir, occ_block * n_vir)
    density = lax.dot_general(
        j_flat,
        amplitude,
        (((1,), (1,)), ((), ())),
        precision=highest,
        preferred_element_type=jnp.float32,
    )
    density = density.reshape(n_auxfun, occ_block, n_vir)
    return lax.all_to_all(density, "aux", split_axis=0, concat_axis=1, tiled=True)


def solution(mesh):
    in_specs = (P("aux", "grp", None), P(), P(), P(), P())
    out_specs = P("aux", "grp", None)
    return jax.shard_map(body, mesh=mesh, in_specs=in_specs, out_specs=out_specs, check_vma=False)
```

profile of v0, /device:TPU:49, one launch (start us, length us, event | category | flops | bytes accessed | tf_op | source)
XLA Modules:
  0.0 460.2 jit_solution(16374623665961684947)
XLA Ops:
  6.5 0.0 copy-start
  6.5 0.0 all-reduce.2.cloned.1.call-start
  6.5 5.1 %copy.16 = f32[96,32,384]{2,0,1:T(8,128)S(1)} copy(f32[96,32,384]{2,1,0:T(8,128)} %param.5) | data formatting | bytes 9437184 | tf_op args[0]
  11.6 58.7 %all_to_all.36 = f32[96,32,384]{2,0,1:T(8,128)S(1)} all-to-all(f32[96,32,384]{2,0,1:T(8,128)S(1)} %copy.16), channel_id=1, replica_groups=mesh['grp'=8,'aux'=16] {'aux'}, dimensions={1} | all-to-all | bytes 9437184 | tf_op jit(solution)/shard_map/all_to_all | solution.py:28
  70.3 3.6 copy.32
  74.0 0.0 copy-start.2
  74.0 0.0 copy-start.5
  74.0 3.2 copy.18
  77.2 0.4 copy-done.2
  77.6 1.2 collective-permute-start
  78.8 0.0 copy-done.5
  78.8 0.6 constant_dynamic-slice_fusion
  80.1 104.5 %collective-permute-done = f32[1536,2,384]{2,0,1:T(8,128)} collective-permute-done((f32[1536,2,384]{2,0,1:T(8,128)}, f32[1536,2,384]{2,0,1:T(8,128)}, u32[]{:S(2)}, u32[]{:S(2)}) %collective-permute-start) | collective-permute-done | bytes 4718624 | tf_op jit(solution)/shard_map/ppermute | solution.py:12
  184.7 2.5 broadcast_select_fusion
  187.2 0.0 all-reduce.2.cloned.1.call-update
  187.8 0.0 copy-done
  187.8 0.2 fusion.15
  188.1 0.1 fusion.20
  188.2 0.1 broadcast_add_fusion
  188.4 0.1 broadcast_subtract_fusion
  188.5 4.9 %copy.25 = f32[192,8,2,384]{3,1,2,0:T(8,128)} copy(f32[192,8,2,384]{3,2,1,0:T(2,128)} %bitcast.36) | data formatting | bytes 9437184
  193.4 126.2 %all-reduce.2.cloned.1.call-done = f32[1536,2,384]{2,0,1:T(8,128)} async-done(((f32[1536,2,384]{2,0,1:T(8,128)}), f32[1536,2,384]{2,0,1:T(8,128)}) %all-reduce.2.cloned.1.call-update) | async-done | bytes 4718608 | tf_op jit(solution)/shard_map/psum | solution.py:17
  319.6 6.0 %copy.19 = f32[1536,2,384]{0,2,1:T(8,128)} copy(f32[1536,2,384]{2,0,1:T(8,128)} %all-reduce.2.cloned.1.call-done) | data formatting | bytes 9437184 | tf_op jit(solution)/shard_map/psum | solution.py:17
  325.6 16.0 %convolution_bitcast_fusion = f32[768,768]{0,1:T(8,128)} fusion(f32[1536,768]{0,1:T(8,128)} %bitcast.40, f32[1536,768]{1,0:T(8,128)} %bitcast.39), kind=kOutput, calls=%fused_computation.10 | convolution fusion | flops 10871635968 | bytes 11796480 | tf_op jit(solution)/shard_map/dot_general | solution.py:48
  341.6 2.9 reshape.57
  344.6 3.5 copy.20
  348.1 15.1 %fusion.2 = f32[1536,2,384]{2,0,1:T(8,128)S(1)} fusion(f32[1536,2,384]{2,0,1:T(8,128)} %all-reduce.2.cloned.1.call-done, f32[2,384,2,384]{1,0,3,2:T(2,128)S(1)} %reshape.57, f32[2,384,2,384]{3,1,2,0:T(8,128)} %copy.20, f32[2]{0:T(128)S(1)} %get-tuple-element.8, f32[2,384,384]{2,1,0:T(8,128)S(1)} %broadcast_subtract_fusion), kind=kOutput, calls=%fused_computation.2 | convolution fusion | flops 10874585088 | bytes 15335432 | tf_op jit(solution)/shard_map/dot_general | solution.py:59
  363.1 19.2 %copy.22 = f32[1536,2,384]{2,1,0:T(2,128)S(1)} copy(f32[1536,2,384]{2,0,1:T(8,128)S(1)} %fusion.2) | data formatting | bytes 9437184 | tf_op jit(solution)/shard_map/dot_general | solution.py:59
  382.4 59.3 %all_to_all.37 = f32[1536,2,384]{2,1,0:T(2,128)S(1)} all-to-all(f32[1536,2,384]{2,1,0:T(2,128)S(1)} %copy.22), channel_id=1, replica_groups=mesh['grp'=8,'aux'=16] {'aux'}, dimensions={0} | all-to-all | bytes 9437184 | tf_op jit(solution)/shard_map/all_to_all | solution.py:67
  441.7 4.8 %copy.23 = f32[96,16,2,384]{3,2,1,0:T(2,128)} copy(f32[96,16,2,384]{3,2,0,1:T(2,128)S(1)} %bitcast.38) | data formatting | bytes 9437184 | tf_op jit(solution)/shard_map/all_to_all | solution.py:67
  446.5 6.9 %all_to_all.33 = f32[96,32,384]{2,1,0:T(8,128)} reshape(f32[96,16,2,384]{3,2,1,0:T(2,128)} %copy.23) | data formatting | bytes 9437184 | tf_op jit(solution)/shard_map/all_to_all | solution.py:67
  453.4 0.0 copy-done.1
  (5 shorter events, 0.0 us)
Async XLA Ops:
  6.5 181.3 %copy-start = (f32[256]{0:T(256)S(1)}, f32[256]{0:T(256)}, u32[]{:S(2)}) copy-start(f32[256]{0:T(256)} %param.6) | copy-start | bytes 3076
  6.5 313.1 %all-reduce.2.cloned.1.call-start = ((), (), s32[]{:S(2)}) async-start(), calls=%async_computation.2 | async-start | bytes 9437184 | tf_op jit(solution)/shard_map/psum | solution.py:17
  74.0 3.6 copy-start.2
  74.0 4.9 %copy-start.5 = (s32[1,8]{1,0:T(1,128)S(1)}, s32[1,8]{1,0:T(1,128)}, u32[]{:S(2)}) copy-start(s32[1,8]{1,0:T(1,128)} %param.9) | copy-start | bytes 100
  77.6 107.0 %collective-permute-start = (f32[1536,2,384]{2,0,1:T(8,128)}, f32[1536,2,384]{2,0,1:T(8,128)}, u32[]{:S(2)}, u32[]{:S(2)}) collective-permute-start(f32[1536,2,384]{2,0,1:T(8,128)} %bitcast.3), channel_id=1, source_target_pairs={{112,0},{0,16},{16,32},{32,48},{48,64},{64,80},{80,96},{96,112},{1... | collective-permute-start | bytes 14155784 | tf_op jit(solution)/shard_map/ppermute | solution.py:12
  187.2 0.7 copy-start.4
  187.2 1.1 copy-start.3
  441.7 11.7 %copy-start.1 = (f32[256]{0:T(256)S(1)}, f32[256]{0:T(256)}, u32[]{:S(2)}) copy-start(f32[256]{0:T(256)} %param.6) | copy-start | bytes 3076
Sparse Core Ops, SparseCore 0:
  187.3 132.2 all-reduce.1
where the time goes:
time: 464 us; the launch traced here: 460 us
  waiting for transfers between devices  231 us (50%)
  blocking collectives  118 us (25%)
  local copies, waits for them, and re-layouts  61.4 us (13%)
  matrix products  31.3 us (7%)
  between operations  14.8 us (3%)
    psum x1, waiting for transfers between devices, from_root(): return lax.psum(kept, axis)  126 us
    ppermute x1, waiting for transfers between devices, from_behind(): return lax.ppermute(block, axis, route)  105 us
    all_to_all x1, blocking collectives, body(): lax.all_to_all(density, 'aux', split_axis=0, concat_axis=1, tiled=True)  59.3 us
    all_to_all x1, blocking collectives, body(): lax.all_to_all(integrals, 'aux', split_axis=1, concat_axis=0, tiled=True)  58.7 us
    dot_general x1, local copies, waits for them, and re-layouts, body(): lax.dot_general(j_flat, amplitude, (((1,), (1,)), ((), ())), precision=hi...  19.2 us
    dot_general x1, matrix products, body(): lax.dot_general(mine_flat, j_flat, (((0,), (0,)), ((), ())), precision=hi...  16 us
    dot_general x1, matrix products, body(): lax.dot_general(j_flat, amplitude, (((1,), (1,)), ((), ())), precision=hi...  15.1 us
    all_to_all x2, local copies, waits for them, and re-layouts, body(): lax.all_to_all(density, 'aux', split_axis=0, concat_axis=1, tiled=True)  11.7 us
  transfers between devices with their start and end apart: 2, of which 2 were waited for; matrix products, arithmetic and copies ran while one was open for 1% of the time, Pallas kernels for 0%

commit v1 on v0

v1 whole, which is shorter than its diff:
```python
import jax
import jax.numpy as jnp
from jax import lax
from jax.sharding import PartitionSpec as P

level_shift = 0.5


def body(integrals, occ_energy, vir_energy, orbital_order, owners):
    highest = lax.Precision.HIGHEST
    high = lax.Precision.HIGH
    n_groups = lax.axis_size("grp")
    n_aux = lax.axis_size("aux")
    grp_index = lax.axis_index("grp")
    aux_index = lax.axis_index("aux")
    group_occ = integrals.shape[1]
    n_vir = integrals.shape[2]
    n_occ = occ_energy.shape[0]
    occ_block = group_occ // n_aux
    owner_now = owners[0, grp_index]
    next_owner = owners[0, (grp_index + 1) % n_groups]
    cut = lax.dynamic_slice_in_dim(integrals, next_owner * occ_block, occ_block, 1)
    cut = lax.ppermute(cut, "grp", [(i, (i + 1) % n_groups) for i in range(n_groups)])
    j_block = lax.all_gather(cut, "aux", axis=0, tiled=True)
    owned = lax.all_to_all(integrals, "aux", split_axis=1, concat_axis=0, tiled=True)
    n_auxfun = owned.shape[0]
    mine_flat = owned.reshape(n_auxfun, occ_block * n_vir)
    onehot = (orbital_order[:, None] == jnp.arange(n_occ, dtype=jnp.int32)[None, :]).astype(
        jnp.float32
    )
    levels = jnp.dot(onehot, occ_energy, precision=highest, preferred_element_type=jnp.float32)
    mine_start = grp_index * group_occ + aux_index * occ_block
    mine_levels = lax.dynamic_slice_in_dim(levels, mine_start, occ_block, 0)
    source_group = (grp_index + n_groups - 1) % n_groups
    vir_pair = vir_energy[None, :, None, None] + vir_energy[None, None, None, :]
    j_flat = j_block.reshape(n_auxfun, occ_block * n_vir)
    j_levels = lax.dynamic_slice_in_dim(
        levels, source_group * group_occ + owner_now * occ_block, occ_block, 0
    )
    pair_flat = lax.dot_general(
        mine_flat, j_flat, (((0,), (0,)), ((), ())), precision=high,
        preferred_element_type=jnp.float32,
    )
    pair_ints = pair_flat.reshape(occ_block, n_vir, occ_block, n_vir)
    swapped = jnp.transpose(pair_ints, (0, 3, 2, 1))
    gaps = vir_pair - mine_levels[:, None, None, None] - j_levels[None, None, :, None] + level_shift
    amplitude = ((2.0 * pair_ints - swapped) / gaps).reshape(occ_block * n_vir, occ_block * n_vir)
    density = lax.dot_general(
        j_flat, amplitude, (((1,), (1,)), ((), ())), precision=high,
        preferred_element_type=jnp.float32,
    )
    density = density.reshape(n_auxfun, occ_block, n_vir)
    return lax.all_to_all(density, "aux", split_axis=0, concat_axis=1, tiled=True)


def solution(mesh):
    in_specs = (P("aux", "grp", None), P(), P(), P(), P())
    out_specs = P("aux", "grp", None)
    return jax.shard_map(body, mesh=mesh, in_specs=in_specs, out_specs=out_specs, check_vma=False)
```

time: 464 us -> 258 us (0.56)
  waiting for transfers between devices: 231 us -> 91 us
  blocking collectives: 118 us -> 58.2 us
  matrix products: 31.3 us -> 19.7 us
  starting transfers between devices: 1.21 us -> 8.15 us
    psum x1 -> x0, waiting for transfers between devices: 126 us -> none  [from_root(): return lax.psum(kept, axis)]
    ppermute x1, waiting for transfers between devices: 105 us -> 10.3 us  [body(): lax.ppermute(cut, 'grp', [(i, (i + 1) % n_groups) for i in range(n_groups)])]
    all_to_all x0 -> x1, waiting for transfers between devices: none -> 80.7 us  [body(): lax.all_to_all(integrals, 'aux', split_axis=1, concat_axis=0, tiled=True)]
    all_to_all x1 -> x0, blocking collectives: 58.7 us -> none  [body(): lax.all_to_all(integrals, 'aux', split_axis=1, concat_axis=0, tiled=True)]
    all_to_all x0 -> x1, starting transfers between devices: none -> 6.87 us  [body(): lax.all_to_all(integrals, 'aux', split_axis=1, concat_axis=0, tiled=True)]
    dot_general x1, matrix products: 15.1 us -> 9.02 us  [body(): lax.dot_general(j_flat, amplitude, (((1,), (1,)), ((), ())), precision=hi...]
    psum x1 -> x0, local copies, waits for them, and re-layouts: 6.04 us -> none  [from_root(): return lax.psum(kept, axis)]
    all_gather x0 -> x1, local copies, waits for them, and re-layouts: none -> 6.04 us  [body(): j_block = lax.all_gather(cut, 'aux', axis=0, tiled=True)]
  transfers between devices with their start and end apart: 2 -> 3, of which waited for: 2 -> 2; matrix products, arithmetic and copies ran while one was open for 1% -> 4% of each run, Pallas kernels for 0% -> 0%
where the time goes in v1:
time: 258 us; the launch traced here: 254 us
  waiting for transfers between devices  91 us (35%)
  local copies, waits for them, and re-layouts  62.1 us (24%)
  blocking collectives  58.2 us (23%)
  matrix products  19.7 us (8%)
  between operations  14.8 us (6%)
  starting transfers between devices  8.15 us (3%)
    all_to_all x1, waiting for transfers between devices, body(): lax.all_to_all(integrals, 'aux', split_axis=1, concat_axis=0, tiled=True)  80.7 us
    all_to_all x1, blocking collectives, body(): lax.all_to_all(density, 'aux', split_axis=0, concat_axis=1, tiled=True)  58.2 us
    dot_general x1, local copies, waits for them, and re-layouts, body(): lax.dot_general(j_flat, amplitude, (((1,), (1,)), ((), ())), precision=hi...  19 us
    all_to_all x2, local copies, waits for them, and re-layouts, body(): lax.all_to_all(density, 'aux', split_axis=0, concat_axis=1, tiled=True)  11.7 us
    unnamed x10, local copies, waits for them, and re-layouts  10.5 us
    dot_general x1, matrix products, body(): lax.dot_general(mine_flat, j_flat, (((0,), (0,)), ((), ())), precision=hi...  10.5 us
    ppermute x1, waiting for transfers between devices, body(): lax.ppermute(cut, 'grp', [(i, (i + 1) % n_groups) for i in range(n_groups)])  10.3 us
    dot_general x1, matrix products, body(): lax.dot_general(j_flat, amplitude, (((1,), (1,)), ((), ())), precision=hi...  9.02 us
  transfers between devices with their start and end apart: 3, of which 2 were waited for; matrix products, arithmetic and copies ran while one was open for 4% of the time, Pallas kernels for 0%

profile of v1, /device:TPU:49, one launch (start us, length us, event | category | flops | bytes accessed | tf_op | source)
XLA Modules:
  0.0 254.3 jit_solution(9069677336525645644)
XLA Ops:
  6.5 0.0 copy-start
  6.5 0.0 all-gather.2.cloned.1.call-start
  6.5 1.4 constant_dynamic-slice_fusion
  8.6 7.3 %copy.16 = f32[96,32,384]{2,0,1:T(8,128)} copy(f32[96,32,384]{2,1,0:T(8,128)} %param.5) | data formatting | bytes 9437184 | tf_op args[0]
  15.8 1.0 constant_dynamic-slice_fusion.1
  16.8 1.3 collective-permute-start
  18.1 10.3 %collective-permute-done = f32[96,2,384]{2,0,1:T(8,128)S(1)} collective-permute-done((f32[96,2,384]{2,0,1:T(8,128)S(1)}, f32[96,2,384]{2,0,1:T(8,128)S(1)}, u32[]{:S(2)}, u32[]{:S(2)}) %collective-permute-start) | collective-permute-done | bytes 294944 | tf_op jit(solution)/shard_map/ppermute | solution.py:23
  28.4 0.0 copy-start.1
  28.4 0.7 copy-done.1
  29.1 0.0 all-gather.2.cloned.1.call-update
  29.1 0.0 copy-start.3
  29.1 0.0 copy-start.2
  29.2 6.9 %all-to-all-start = ((f32[96,32,384]{2,0,1:T(8,128)}), f32[96,32,384]{2,0,1:T(8,128)}, u32[]{:S(2)}, u32[]{:S(2)}) async-start(f32[96,32,384]{2,0,1:T(8,128)} %copy.16), calls=%async_computation | async-start | bytes 9437184 | tf_op jit(solution)/shard_map/all_to_all | solution.py:25
  36.7 0.0 copy-done
  36.7 0.0 copy-done.3
  36.7 0.2 fusion.15
  36.9 0.1 fusion.19
  37.1 0.0 copy-done.2
  37.1 0.1 broadcast_add_fusion
  37.2 0.1 broadcast_subtract_fusion
  37.4 80.7 %all-to-all-done = f32[96,32,384]{2,0,1:T(8,128)} async-done(((f32[96,32,384]{2,0,1:T(8,128)}), f32[96,32,384]{2,0,1:T(8,128)}, u32[]{:S(2)}, u32[]{:S(2)}) %all-to-all-start) | async-done | bytes 4718624 | tf_op jit(solution)/shard_map/all_to_all | solution.py:25
  118.1 6.0 %copy.19 = f32[96,16,2,384]{3,2,0,1:T(2,128)S(1)} copy(f32[96,16,2,384]{3,0,2,1:T(8,128)} %bitcast.3) | data formatting | bytes 9437184 | tf_op jit(solution)/shard_map/all_to_all | solution.py:25
  124.1 2.5 copy.25
  126.6 6.0 %copy.17 = f32[1536,2,384]{0,2,1:T(8,128)} copy(f32[1536,2,384]{2,0,1:T(8,128)} %all-gather.2.cloned.1.call-done) | data formatting | bytes 9437184 | tf_op jit(solution)/shard_map/all_gather | solution.py:24
  132.6 10.5 %convolution_bitcast_fusion = f32[768,768]{0,1:T(8,128)} fusion(f32[1536,768]{0,1:T(8,128)} %bitcast.37, f32[1536,768]{1,0:T(8,128)} %bitcast.36), kind=kOutput, calls=%fused_computation.9 | convolution fusion | flops 5435817984 | bytes 11796480 | tf_op jit(solution)/shard_map/dot_general | solution.py:40
  143.1 2.9 %reshape.60 = f32[2,384,2,384]{1,0,3,2:T(2,128)S(1)} reshape(f32[768,768]{0,1:T(8,128)} %convolution_bitcast_fusion) | data formatting | bytes 4718592 | tf_op jit(solution)/shard_map/reshape | solution.py:44
  146.0 3.5 %copy.20 = f32[2,384,2,384]{3,1,2,0:T(8,128)} copy(f32[2,384,2,384]{1,0,3,2:T(2,128)S(1)} %reshape.60) | data formatting | bytes 4718592 | tf_op jit(solution)/shard_map/reshape | solution.py:44
  149.5 9.0 %fusion.2 = f32[1536,2,384]{2,0,1:T(8,128)S(1)} fusion(f32[1536,2,384]{2,0,1:T(8,128)} %all-gather.2.cloned.1.call-done, f32[2,384,2,384]{1,0,3,2:T(2,128)S(1)} %reshape.60, f32[2,384,2,384]{3,1,2,0:T(8,128)} %copy.20, f32[2]{0:T(128)S(1)} %get-tuple-element.6, f32[2,384,384]{2,1,0:T(8,128)S(1)} %broadcast_subtract_fusion), kind=kOutput, calls=%fused_computation.2 | convolution fusion | flops 5438767104 | bytes 15335432 | tf_op jit(solution)/shard_map/dot_general | solution.py:48
  158.5 19.0 %copy.22 = f32[1536,2,384]{2,1,0:T(2,128)S(1)} copy(f32[1536,2,384]{2,0,1:T(8,128)S(1)} %fusion.2) | data formatting | bytes 9437184 | tf_op jit(solution)/shard_map/dot_general | solution.py:48
  177.5 58.2 %all_to_all.33 = f32[1536,2,384]{2,1,0:T(2,128)S(1)} all-to-all(f32[1536,2,384]{2,1,0:T(2,128)S(1)} %copy.22), channel_id=1, replica_groups=mesh['grp'=8,'aux'=16] {'aux'}, dimensions={0} | all-to-all | bytes 9437184 | tf_op jit(solution)/shard_map/all_to_all | solution.py:53
  235.8 4.8 %copy.23 = f32[96,16,2,384]{3,2,1,0:T(2,128)} copy(f32[96,16,2,384]{3,2,0,1:T(2,128)S(1)} %bitcast.35) | data formatting | bytes 9437184 | tf_op jit(solution)/shard_map/all_to_all | solution.py:53
  240.6 6.9 %all_to_all.30 = f32[96,32,384]{2,1,0:T(8,128)} reshape(f32[96,16,2,384]{3,2,1,0:T(2,128)} %copy.23) | data formatting | bytes 9437184 | tf_op jit(solution)/shard_map/all_to_all | solution.py:53
  (1 shorter events, 0.0 us)
Async XLA Ops:
  6.5 30.1 %copy-start = (f32[256]{0:T(256)S(1)}, f32[256]{0:T(256)}, u32[]{:S(2)}) copy-start(f32[256]{0:T(256)} %param.6) | copy-start | bytes 3076
  6.5 120.0 %all-gather.2.cloned.1.call-start = ((), (), s32[]{:S(2)}) async-start(), calls=%async_computation.2 | async-start | bytes 5013504 | tf_op jit(solution)/shard_map/all_gather | solution.py:24
  16.8 11.6 %collective-permute-start = (f32[96,2,384]{2,0,1:T(8,128)S(1)}, f32[96,2,384]{2,0,1:T(8,128)S(1)}, u32[]{:S(2)}, u32[]{:S(2)}) collective-permute-start(f32[96,2,384]{2,0,1:T(8,128)S(1)} %constant_dynamic-slice_fusion.1), channel_id=1, source_target_pairs={{0,16},{16,32},{32,48},{48,64},{64,80},{80,96},{96,112},{112,0},{1... | collective-permute-start | bytes 884744 | tf_op jit(solution)/shard_map/ppermute | solution.py:23
  28.4 0.7 copy-start.1
  29.1 7.5 %copy-start.3 = (s32[256]{0:T(256)S(1)}, s32[256]{0:T(256)}, u32[]{:S(2)}) copy-start(s32[256]{0:T(256)} %param.8) | copy-start | bytes 3076
  29.1 7.9 %copy-start.2 = (f32[384]{0:T(512)S(1)}, f32[384]{0:T(512)}, u32[]{:S(2)}) copy-start(f32[384]{0:T(512)} %param.7) | copy-start | bytes 4612
  29.2 88.9 %all-to-all-start = ((f32[96,32,384]{2,0,1:T(8,128)}), f32[96,32,384]{2,0,1:T(8,128)}, u32[]{:S(2)}, u32[]{:S(2)}) async-start(f32[96,32,384]{2,0,1:T(8,128)} %copy.16), calls=%async_computation | async-start | bytes 9437184 | tf_op jit(solution)/shard_map/all_to_all | solution.py:25
Sparse Core Ops, SparseCore 0:
  29.3 85.7 all-gather.1

commit v2 on v1

v2 whole, which is shorter than its diff:
```python
import jax
import jax.numpy as jnp
from jax import lax
from jax.experimental import pallas as pl
from jax.experimental.pallas import tpu as pltpu
from jax.sharding import PartitionSpec as P

level_shift = 0.5
MESH = pl.DeviceIdType.MESH

ROUTE = (
    (1, 0, 0), (3, 1, 0), (2, 1, 0), (0, 1, 0), (2, 0, 0),
    (1, 1, 0), (3, 0, 0), (0, 0, 1), (1, 0, 1), (3, 1, 1),
    (2, 1, 1), (0, 1, 1), (2, 0, 1), (1, 1, 1), (3, 0, 1),
)


def split(x):
    hi = x.astype(jnp.bfloat16)
    lo = (x - hi.astype(jnp.float32)).astype(jnp.bfloat16)
    return hi, lo


def kernel(sizes, occ, order, owners, vir, in_hbm, out, rows_in, staged, held, jblock, jcut, jhi, jlo,
           jthi, jtlo, xhi, xlo, acc, ahi, alo, vsum, dens, back, load_sem, jsend, jrecv, xsend, xrecv,
           osend, orecv):
    n_grp, n_aux, depth, n_occ, n_vir, occ_block = sizes
    chunk = 4 * depth
    grp = lax.axis_index("grp")
    me = lax.axis_index("aux")
    y, z, c = lax.div(me, 4), lax.rem(lax.div(me, 2), 2), lax.rem(me, 2)
    nxt = lax.rem(grp + 1, n_grp)
    prv = lax.rem(grp + n_grp - 1, n_grp)

    def dev(dy, dz, dc):
        return lax.rem(y + dy, 4) * 4 + lax.rem(z + dz, 2) * 2 + lax.rem(c + dc, 2)

    def rows(a):
        return pl.ds(pl.multiple_of(a * depth, 8), depth)

    lanes = range(n_vir // 128)
    loads = [pltpu.make_async_copy(in_hbm.at[:, n * 128:(n + 1) * 128], rows_in.at[n], load_sem.at[n]) for n in lanes]
    for load in loads:
        load.start()
    barrier = pltpu.get_barrier_semaphore()
    for n in range(1, 16):
        pl.semaphore_signal(barrier, inc=1, device_id=(grp, lax.rem(me + n, 16)), device_id_type=MESH)
    pl.semaphore_signal(barrier, inc=1, device_id=(nxt, me), device_id_type=MESH)
    pl.semaphore_signal(barrier, inc=1, device_id=(prv, me), device_id_type=MESH)

    wide = jnp.broadcast_to(vir[...], (n_vir, n_vir))
    vsum[...] = wide + wide.T
    for load in loads:
        load.wait()

    picked = owners[0, nxt] * occ_block
    for k in range(occ_block):
        for n in lanes:
            at = k * n_vir + n * 128
            jcut[:, at:at + 128] = rows_in[n, pl.ds(picked + k, depth, stride=n_occ), :]
    pl.semaphore_wait(barrier, 17)

    def jcopy(n, a, target, src=None):
        return pltpu.make_async_remote_copy(
            src_ref=jblock.at[rows(a), :] if src is None else src, dst_ref=jblock.at[rows(a), :],
            send_sem=jsend.at[n], recv_sem=jrecv.at[a], device_id=target, device_id_type=MESH)

    def xcopy(k, n, a, target):
        return pltpu.make_async_remote_copy(
            src_ref=staged.at[k, rows(target), :], dst_ref=held.at[k, rows(a), :],
            send_sem=xsend.at[k, n], recv_sem=xrecv.at[k, a], device_id=(grp, target), device_id_type=MESH)

    def ocopy(k, n, a, target):
        return pltpu.make_async_remote_copy(
            src_ref=dens.at[k, rows(target), :], dst_ref=back.at[k, rows(a), :],
            send_sem=osend.at[k, n], recv_sem=orecv.at[k, a], device_id=(grp, target), device_id_type=MESH)

    for d in range(n_aux):
        for k in range(occ_block):
            for n in lanes:
                staged[k, d * depth:(d + 1) * depth, n * 128:(n + 1) * 128] = rows_in[
                    n, pl.ds(d * occ_block + k, depth, stride=n_occ), :]
        if d == 0:
            jcopy(0, me, (nxt, me), jcut).start()
    for k in range(occ_block):
        held[k, rows(me), :] = staged[k, rows(me), :]

    xorder = [(k, n) for k in range(occ_block) for n in range(len(ROUTE))]
    xplace = [0]

    def xsend_some(count):
        for k, n in xorder[xplace[0]:xplace[0] + count]:
            xcopy(k, n, me, dev(*ROUTE[n])).start()
        xplace[0] += count

    steps = [0]
    up, down, over, twin = dev(1, 0, 0), dev(3, 0, 0), dev(0, 1, 0), dev(0, 0, 1)
    sent = []

    def jrelay(a, targets):
        jcopy(0, a, (grp, twin)).wait_recv()
        for t in tuple(targets) + (twin,):
            steps[0] += 1
            copy = jcopy(steps[0], a, (grp, t))
            copy.start()
            sent.append(copy)

    xsend_some(4)
    jrelay(me, (over, up, down))
    xsend_some(3)
    jrelay(over, (up, down))
    xsend_some(3)
    jrelay(down, (up,))
    jrelay(dev(1, 1, 0), (down,))
    xsend_some(5)
    jrelay(up, ())
    jrelay(dev(3, 1, 0), ())
    xsend_some(15)
    jrelay(dev(2, 0, 0), ())
    jrelay(dev(2, 1, 0), ())

    def prepare(q, _):
        for zz in range(2):
            a = q * 4 + zz * 2 + lax.rem(c + 1, 2)
            jcopy(0, a, (grp, twin)).wait_recv()
        base = pl.multiple_of(q * chunk, 128)
        here = pl.ds(base, chunk)
        for m in range(chunk // 128):
            part = pl.ds(pl.multiple_of(base + m * 128, 128), 128)
            hi, lo = split(jblock[part, :])
            jhi[part, :] = hi
            jlo[part, :] = lo
        for n in range(occ_block * n_vir // 128):
            hi, lo = split(jblock[here, n * 128:(n + 1) * 128].T)
            jthi[q, n * 128:(n + 1) * 128, :] = hi
            jtlo[q, n * 128:(n + 1) * 128, :] = lo
        return 0

    lax.fori_loop(0, 4, prepare, 0)

    def half(k, _):
        acc[...] = jnp.zeros_like(acc)

        def first(q, _):
            for m in range(4):
                a = q * 4 + m

                @pl.when(a != me)
                def _():
                    xcopy(k, 0, a, twin).wait_recv()
            for m in range(4):
                hi, lo = split(held[k, rows(q * 4 + m), :])
                xhi[m * depth:(m + 1) * depth, :] = hi
                xlo[m * depth:(m + 1) * depth, :] = lo
            acc[...] += jnp.dot(jthi[q], xhi[...], preferred_element_type=jnp.float32)
            acc[...] += jnp.dot(jthi[q], xlo[...], preferred_element_type=jnp.float32)
            acc[...] += jnp.dot(jtlo[q], xhi[...], preferred_element_type=jnp.float32)
            return 0

        lax.fori_loop(0, 4, first, 0)
        level_i = occ[order[grp * n_occ + me * occ_block + k]]

        def amplitude(j, _):
            level_j = occ[order[prv * n_occ + owners[0, grp] * occ_block + j]]
            shift = level_shift - level_i - level_j
            for b in range(n_vir // 128):
                for a in range(n_vir // 128):
                    one = acc[pl.ds(pl.multiple_of(j * n_vir + b * 128, 128), 128), a * 128:(a + 1) * 128]
                    two = acc[pl.ds(pl.multiple_of(j * n_vir + a * 128, 128), 128), b * 128:(b + 1) * 128]
                    gap = vsum[b * 128:(b + 1) * 128, a * 128:(a + 1) * 128] + shift
                    hi, lo = split((2.0 * one - two.T) / gap)
                    at = pl.ds(pl.multiple_of(j * n_vir + b * 128, 128), 128)
                    ahi[at, a * 128:(a + 1) * 128] = hi
                    alo[at, a * 128:(a + 1) * 128] = lo
            return 0

        lax.fori_loop(0, occ_block, amplitude, 0)

        def second(q, _):
            here = pl.ds(pl.multiple_of(q * chunk, 128), chunk)
            part = jnp.dot(jhi[here, :], ahi[...], preferred_element_type=jnp.float32)
            part += jnp.dot(jhi[here, :], alo[...], preferred_element_type=jnp.float32)
            part += jnp.dot(jlo[here, :], ahi[...], preferred_element_type=jnp.float32)
            dens[k, here, :] = part
            return 0

        lax.fori_loop(0, 4, second, 0)
        back[k, rows(me), :] = dens[k, rows(me), :]
        for n, step in enumerate(ROUTE):
            ocopy(k, n, me, dev(*step)).start()
        return 0

    lax.fori_loop(0, occ_block, half, 0)

    for k in range(occ_block):
        for a in range(n_aux):
            @pl.when(a != me)
            def _():
                ocopy(k, 0, a, twin).wait_recv()
            for n in lanes:
                out[n, pl.ds(a * occ_block + k, depth, stride=n_occ), :] = back[
                    k, a * depth:(a + 1) * depth, n * 128:(n + 1) * 128]

    jcopy(0, me, (nxt, me), jcut).wait_send()
    for copy in sent:
        copy.wait_send()
    for k in range(occ_block):
        for n, step in enumerate(ROUTE):
            xcopy(k, n, me, dev(*step)).wait_send()
            ocopy(k, n, me, dev(*step)).wait_send()


def body(integrals, occ_energy, vir_energy, orbital_order, owners):
    n_grp = lax.axis_size("grp")
    n_aux = lax.axis_size("aux")
    depth, n_occ, n_vir = integrals.shape
    occ_block = n_occ // n_aux
    total = depth * n_aux
    jb = occ_block * n_vir
    f32, bf16 = jnp.float32, jnp.bfloat16
    sizes = (n_grp, n_aux, depth, n_occ, n_vir, occ_block)
    smem = pl.BlockSpec(memory_space=pltpu.SMEM)
    vmem = pl.BlockSpec(memory_space=pltpu.VMEM)
    out = pl.pallas_call(
        lambda *refs: kernel(sizes, *refs),
        out_shape=jax.ShapeDtypeStruct((n_vir // 128, depth * n_occ, 128), f32),
        in_specs=[smem, smem, smem, vmem, pl.BlockSpec(memory_space=pl.ANY)],
        out_specs=vmem,
        scratch_shapes=[
            pltpu.VMEM((n_vir // 128, depth * n_occ, 128), f32),
            pltpu.VMEM((occ_block, total, n_vir), f32),
            pltpu.VMEM((occ_block, total, n_vir), f32),
            pltpu.VMEM((total, jb), f32),
            pltpu.VMEM((depth, jb), f32),
            pltpu.VMEM((total, jb), bf16),
            pltpu.VMEM((total, jb), bf16),
            pltpu.VMEM((4, jb, 4 * depth), bf16),
            pltpu.VMEM((4, jb, 4 * depth), bf16),
            pltpu.VMEM((4 * depth, n_vir), bf16),
            pltpu.VMEM((4 * depth, n_vir), bf16),
            pltpu.VMEM((jb, n_vir), f32),
            pltpu.VMEM((jb, n_vir), bf16),
            pltpu.VMEM((jb, n_vir), bf16),
            pltpu.VMEM((n_vir, n_vir), f32),
            pltpu.VMEM((occ_block, total, n_vir), f32),
            pltpu.VMEM((occ_block, total, n_vir), f32),
            pltpu.SemaphoreType.DMA((n_vir // 128,)),
            pltpu.SemaphoreType.DMA((24,)),
            pltpu.SemaphoreType.DMA((n_aux,)),
            pltpu.SemaphoreType.DMA((occ_block, n_aux)),
            pltpu.SemaphoreType.DMA((occ_block, n_aux)),
            pltpu.SemaphoreType.DMA((occ_block, n_aux)),
            pltpu.SemaphoreType.DMA((occ_block, n_aux)),
        ],
        compiler_params=pltpu.CompilerParams(
            collective_id=0, has_side_effects=True, vmem_limit_bytes=63 << 20),
    )(occ_energy, orbital_order, owners, vir_energy.reshape(1, n_vir), integrals.reshape(depth * n_occ, n_vir))
    return jnp.swapaxes(out, 0, 1).reshape(depth, n_occ, n_vir)


def solution(mesh):
    in_specs = (P("aux", "grp", None), P(), P(), P(), P())
    out_specs = P("aux", "grp", None)
    return jax.shard_map(body, mesh=mesh, in_specs=in_specs, out_specs=out_specs, check_vma=False)
```

time: 258 us -> 168 us (0.65); the launches traced: 254 us -> 168 us
  Pallas kernels: 0 us -> 149 us
  waiting for transfers between devices: 91 us -> 0 us
  blocking collectives: 58.2 us -> 0 us
  local copies, waits for them, and re-layouts: 62.1 us -> 18.5 us
  matrix products: 19.7 us -> 0 us
  between operations: 14.8 us -> 0.01 us
  starting transfers between devices: 8.15 us -> 0 us
    pallas_call x0 -> x1, Pallas kernels: none -> 149 us  [body(): pl.pallas_call(lambda *refs: kernel(sizes, *refs), out_shape=jax.ShapeDty...]
    all_to_all x1 -> x0, waiting for transfers between devices: 80.7 us -> none  [body(): lax.all_to_all(integrals, 'aux', split_axis=1, concat_axis=0, tiled=True)]
    all_to_all x1 -> x0, blocking collectives: 58.2 us -> none  [body(): lax.all_to_all(density, 'aux', split_axis=0, concat_axis=1, tiled=True)]
    dot_general x3 -> x0, matrix products: 19.7 us -> none  [the longest x1 10.5 us: body(): lax.dot_general(mine_flat, j_flat, (((0,), (0,)), ((), ())), precision=hi...]
    dot_general x1 -> x0, local copies, waits for them, and re-layouts: 19 us -> none  [body(): lax.dot_general(j_flat, amplitude, (((1,), (1,)), ((), ())), precision=hi...]
    all_to_all x3 -> x0, local copies, waits for them, and re-layouts: 17.7 us -> none  [the longest x2 11.7 us: body(): lax.all_to_all(density, 'aux', split_axis=0, concat_axis=1, tiled=True)]
    unnamed x10 -> x0, local copies, waits for them, and re-layouts: 10.5 us -> none
    ppermute x1 -> x0, waiting for transfers between devices: 10.3 us -> none  [body(): lax.ppermute(cut, 'grp', [(i, (i + 1) % n_groups) for i in range(n_groups)])]
  transfers between devices with their start and end apart: 3 -> 0, of which waited for: 2 -> 0; matrix products, arithmetic and copies ran while one was open for 4% -> 0% of each run, Pallas kernels for 0% -> 0%
where the time goes in v2:
time: 168 us
  Pallas kernels  149 us (89%)
  local copies, waits for them, and re-layouts  18.5 us (11%)
    pallas_call x1, Pallas kernels, body(): pl.pallas_call(lambda *refs: kernel(sizes, *refs), out_shape=jax.ShapeDty...  149 us
    transpose x1, local copies, waits for them, and re-layouts, body(): return jnp.swapaxes(out, 0, 1).reshape(depth, n_occ, n_vir)  8.7 us
    reshape x1, local copies, waits for them, and re-layouts, body(): return jnp.swapaxes(out, 0, 1).reshape(depth, n_occ, n_vir)  8.52 us

profile of v2, /device:TPU:49, one launch (start us, length us, event | category | flops | bytes accessed | tf_op | source)
XLA Modules:
  0.0 167.6 jit_solution(2484600062274608163)
XLA Ops:
  0.0 1.2 reshape.9.refs_3_
  1.2 149.1 %shard_map.55 = f32[3,3072,128]{2,1,0:T(8,128)} custom-call(f32[256]{0:T(256)} %refs_0_.1, s32[256]{0:T(256)} %refs_1_.1, s32[1,8]{1,0:T(1,128)} %refs_2_.1, f32[1,384]{1,0:T(1,128)} %reshape.9.refs_3_, f32[3072,384]{1,0:T(8,128)} %bitcast.3), custom_call_target="tpu_custom_call" | custom-call | tf_op jit(solution)/shard_map/pallas_call | solution.py:224
  150.4 8.7 %copy.6 = f32[3072,3,128]{2,1,0:T(4,128)} copy(f32[3072,3,128]{2,0,1:T(8,128)} %bitcast.2) | data formatting | bytes 9437184 | tf_op jit(solution)/shard_map/transpose | solution.py:258
  159.1 8.5 %reshape.11 = f32[96,32,384]{2,1,0:T(8,128)} reshape(f32[3072,3,128]{2,1,0:T(4,128)} %copy.6) | data formatting | bytes 9437184 | tf_op jit(solution)/shard_map/reshape | solution.py:258

commit v3 on v2

--- a/solution.py
+++ b/solution.py
@@ -7,6 +7,8 @@
 
 level_shift = 0.5
 MESH = pl.DeviceIdType.MESH
+
+PIECES = 3
 
 ROUTE = (
     (1, 0, 0), (3, 1, 0), (2, 1, 0), (0, 1, 0), (2, 0, 0),
@@ -48,7 +50,7 @@
     pl.semaphore_signal(barrier, inc=1, device_id=(nxt, me), device_id_type=MESH)
     pl.semaphore_signal(barrier, inc=1, device_id=(prv, me), device_id_type=MESH)
 
-    wide = jnp.broadcast_to(vir[...], (n_vir, n_vir))
+    wide = jnp.broadcast_to(vir[...][None, :], (n_vir, n_vir))
     vsum[...] = wide + wide.T
     for load in loads:
         load.wait()
@@ -60,10 +62,17 @@
             jcut[:, at:at + 128] = rows_in[n, pl.ds(picked + k, depth, stride=n_occ), :]
     pl.semaphore_wait(barrier, 17)
 
-    def jcopy(n, a, target, src=None):
+    piece = depth // PIECES
+
+    def jcopy(n, p, a, target, src=None):
+        at = pl.ds(pl.multiple_of(a * depth + p * piece, 8), piece)
         return pltpu.make_async_remote_copy(
-            src_ref=jblock.at[rows(a), :] if src is None else src, dst_ref=jblock.at[rows(a), :],
-            send_sem=jsend.at[n], recv_sem=jrecv.at[a], device_id=target, device_id_type=MESH)
+            src_ref=jblock.at[at, :] if src is None else src, dst_ref=jblock.at[at, :],
+            send_sem=jsend.at[n], recv_sem=jrecv.at[p, a], device_id=target, device_id_type=MESH)
+
+    hops = [jcopy(p, p, me, (nxt, me), jcut.at[p * piece:(p + 1) * piece, :]) for p in range(PIECES)]
+    for hop in hops:
+        hop.start()
 
     def xcopy(k, n, a, target):
         return pltpu.make_async_remote_copy(
@@ -75,54 +84,50 @@
             src_ref=dens.at[k, rows(target), :], dst_ref=back.at[k, rows(a), :],
             send_sem=osend.at[k, n], recv_sem=orecv.at[k, a], device_id=(grp, target), device_id_type=MESH)
 
+    xorder = [(k, n) for k in range(occ_block) for n in range(len(ROUTE))]
+
+    def xsend_some(first, last):
+        for k, n in xorder[first:last]:
+            xcopy(k, n, me, dev(*ROUTE[n])).start()
+
+    up, down, over, twin = dev(1, 0, 0), dev(3, 0, 0), dev(0, 1, 0), dev(0, 0, 1)
+    across, beyond, far = dev(1, 1, 0), dev(2, 0, 0), dev(2, 1, 0)
+    behind = dev(3, 1, 0)
+    by_y = ((me, (up, down, over)), (over, (up, down)), (down, (up,)), (across, (down,)),
+            (up, ()), (behind, ()), (beyond, ()), (far, ()))
+    by_z = ((me, (up, down, over)), (down, (over, up)), (up, (over,)), (across, (down,)),
+            (over, ()), (behind, ()), (beyond, ()), (far, ()))
+    plans = (by_z, by_y, by_z)
+    sent = []
+
+    def jrelay(p, event):
+        a, targets = plans[p][event]
+        jcopy(0, p, a, (grp, twin)).wait_recv()
+        for t in targets + (twin,):
+            copy = jcopy(len(sent) + PIECES, p, a, (grp, t))
+            copy.start()
+            sent.append(copy)
+
+    for p, event in ((0, 0), (1, 0), (0, 1), (0, 2), (2, 0), (1, 1), (1, 2), (0, 3), (2, 1), (2, 2), (1, 3), (2, 3)):
+        jrelay(p, event)
     for d in range(n_aux):
         for k in range(occ_block):
             for n in lanes:
                 staged[k, d * depth:(d + 1) * depth, n * 128:(n + 1) * 128] = rows_in[
                     n, pl.ds(d * occ_block + k, depth, stride=n_occ), :]
-        if d == 0:
-            jcopy(0, me, (nxt, me), jcut).start()
     for k in range(occ_block):
         held[k, rows(me), :] = staged[k, rows(me), :]
 
-    xorder = [(k, n) for k in range(occ_block) for n in range(len(ROUTE))]
-    xplace = [0]
-
-    def xsend_some(count):
-        for k, n in xorder[xplace[0]:xplace[0] + count]:
-            xcopy(k, n, me, dev(*ROUTE[n])).start()
-        xplace[0] += count
-
-    steps = [0]
-    up, down, over, twin = dev(1, 0, 0), dev(3, 0, 0), dev(0, 1, 0), dev(0, 0, 1)
-    sent = []
-
-    def jrelay(a, targets):
-        jcopy(0, a, (grp, twin)).wait_recv()
-        for t in tuple(targets) + (twin,):
-            steps[0] += 1
-            copy = jcopy(steps[0], a, (grp, t))
-            copy.start()
-            sent.append(copy)
-
-    xsend_some(4)
-    jrelay(me, (over, up, down))
-    xsend_some(3)
-    jrelay(over, (up, down))
-    xsend_some(3)
-    jrelay(down, (up,))
-    jrelay(dev(1, 1, 0), (down,))
-    xsend_some(5)
-    jrelay(up, ())
-    jrelay(dev(3, 1, 0), ())
-    xsend_some(15)
-    jrelay(dev(2, 0, 0), ())
-    jrelay(dev(2, 1, 0), ())
+    xsend_some(0, 30)
+    for event in range(4, 8):
+        for p in range(PIECES):
+            jrelay(p, event)
 
     def prepare(q, _):
         for zz in range(2):
             a = q * 4 + zz * 2 + lax.rem(c + 1, 2)
-            jcopy(0, a, (grp, twin)).wait_recv()
+            for p in range(PIECES):
+                jcopy(0, p, a, (grp, twin)).wait_recv()
         base = pl.multiple_of(q * chunk, 128)
         here = pl.ds(base, chunk)
         for m in range(chunk // 128):
@@ -201,13 +206,25 @@
                 out[n, pl.ds(a * occ_block + k, depth, stride=n_occ), :] = back[
                     k, a * depth:(a + 1) * depth, n * 128:(n + 1) * 128]
 
-    jcopy(0, me, (nxt, me), jcut).wait_send()
-    for copy in sent:
+    for copy in hops + sent:
         copy.wait_send()
     for k in range(occ_block):
         for n, step in enumerate(ROUTE):
             xcopy(k, n, me, dev(*step)).wait_send()
             ocopy(k, n, me, dev(*step)).wait_send()
+
+
+def write(parts, held, out, sem):
+    lanes, count, _ = held.shape
+    step = count // parts
+    copies = []
+    for p in range(parts):
+        for n in range(lanes):
+            at = pl.ds(p * step, step)
+            copies.append(pltpu.make_async_copy(held.at[n, at, :], out.at[at, n * 128:(n + 1) * 128], sem.at[p, n]))
+            copies[-1].start()
+    for copy in copies:
+        copy.wait()
 
 
 def body(integrals, occ_energy, vir_energy, orbital_order, owners):
@@ -223,7 +240,7 @@
     vmem = pl.BlockSpec(memory_space=pltpu.VMEM)
     out = pl.pallas_call(
         lambda *refs: kernel(sizes, *refs),
-        out_shape=jax.ShapeDtypeStruct((n_vir // 128, depth * n_occ, 128), f32),
+        out_shape=pltpu.VMEM((n_vir // 128, depth * n_occ, 128), f32),
         in_specs=[smem, smem, smem, vmem, pl.BlockSpec(memory_space=pl.ANY)],
         out_specs=vmem,
         scratch_shapes=[
@@ -245,17 +262,26 @@
             pltpu.VMEM((occ_block, total, n_vir), f32),
             pltpu.VMEM((occ_block, total, n_vir), f32),
             pltpu.SemaphoreType.DMA((n_vir // 128,)),
-            pltpu.SemaphoreType.DMA((24,)),
-            pltpu.SemaphoreType.DMA((n_aux,)),
+            pltpu.SemaphoreType.DMA((PIECES * 16,)),
+            pltpu.SemaphoreType.DMA((PIECES, n_aux)),
             pltpu.SemaphoreType.DMA((occ_block, n_aux)),
             pltpu.SemaphoreType.DMA((occ_block, n_aux)),
             pltpu.SemaphoreType.DMA((occ_block, n_aux)),
             pltpu.SemaphoreType.DMA((occ_block, n_aux)),
         ],
         compiler_params=pltpu.CompilerParams(
-            collective_id=0, has_side_effects=True, vmem_limit_bytes=63 << 20),
-    )(occ_energy, orbital_order, owners, vir_energy.reshape(1, n_vir), integrals.reshape(depth * n_occ, n_vir))
-    return jnp.swapaxes(out, 0, 1).reshape(depth, n_occ, n_vir)
+            collective_id=0, has_side_effects=True, vmem_limit_bytes=50 << 20),
+    )(occ_energy, orbital_order, owners, vir_energy, integrals.reshape(depth * n_occ, n_vir))
+    parts = 4
+    out = pl.pallas_call(
+        lambda *refs: write(parts, *refs),
+        out_shape=jax.ShapeDtypeStruct((depth * n_occ, n_vir), f32),
+        in_specs=[vmem],
+        out_specs=pl.BlockSpec(memory_space=pl.ANY),
+        scratch_shapes=[pltpu.SemaphoreType.DMA((parts, n_vir // 128))],
+        compiler_params=pltpu.CompilerParams(vmem_limit_bytes=8 << 20),
+    )(out)
+    return out.reshape(depth, n_occ, n_vir)
 
 
 def solution(mesh):

time: 168 us -> 149 us (0.89)
  the two profiles are of different devices: /device:TPU:49 before, /device:TPU:105 now
where the time goes in v3:
time: 149 us
  Pallas kernels  149 us (100%)
    pallas_call x1, Pallas kernels, body(): pl.pallas_call(lambda *refs: kernel(sizes, *refs), out_shape=pltpu.VMEM((...  147 us

profile of v3, /device:TPU:105, one launch (start us, length us, event | category | flops | bytes accessed | tf_op | source)
XLA Modules:
  0.0 148.8 jit_solution(12644946304702783800)
XLA Ops:
  0.0 146.5 %shard_map.55.refs_0_ = f32[3,3072,128]{2,1,0:T(8,128)S(1)} custom-call(f32[256]{0:T(256)} %refs_0_.1, s32[256]{0:T(256)} %refs_1_.1, s32[1,8]{1,0:T(1,128)} %refs_2_.1, f32[384]{0:T(512)} %refs_3_.1, f32[3072,384]{1,0:T(8,128)} %bitcast.2), custom_call_target="tpu_custom_call" | custom-call | tf_op jit(solution)/shard_map/pallas_call | solution.py:241
  146.5 2.3 %shard_map.56 = f32[3072,384]{1,0:T(8,128)} custom-call(f32[3,3072,128]{2,1,0:T(8,128)S(1)} %shard_map.55.refs_0_), custom_call_target="tpu_custom_call" | custom-call | tf_op jit(solution)/shard_map/pallas_call | solution.py:276

commit v4 on v3

--- a/solution.py
+++ b/solution.py
@@ -9,6 +9,14 @@
 MESH = pl.DeviceIdType.MESH
 
 PIECES = 3
+
+EVENTS = ((0, 0), (1, 0), (0, 1), (0, 2), (2, 0), (1, 1), (1, 2), (0, 3), (2, 1), (2, 2), (1, 3), (2, 3))
+EARLY = (0, 6, 3)
+FILL = (6, 0, 0, 0, 0, 0, 0, 0, 0, 0, 6, 0, 0)
+FIRST = 3
+STAGE = (0, 0, 0, 0, 0, 12, 0, 0, 0, 0, 0, 0, 0)
+
+PARTS = 2
 
 ROUTE = (
     (1, 0, 0), (3, 1, 0), (2, 1, 0), (0, 1, 0), (2, 0, 0),
@@ -37,6 +45,12 @@
     def dev(dy, dz, dc):
         return lax.rem(y + dy, 4) * 4 + lax.rem(z + dz, 2) * 2 + lax.rem(c + dc, 2)
 
+    def swap(group):
+        return 1 - jnp.minimum(lax.rem(group, 4), 1)
+
+    def shard(dy, dz, dc):
+        return dev(dy, dz + swap(grp), dc)
+
     def rows(a):
         return pl.ds(pl.multiple_of(a * depth, 8), depth)
 
@@ -47,8 +61,8 @@
     barrier = pltpu.get_barrier_semaphore()
     for n in range(1, 16):
         pl.semaphore_signal(barrier, inc=1, device_id=(grp, lax.rem(me + n, 16)), device_id_type=MESH)
-    pl.semaphore_signal(barrier, inc=1, device_id=(nxt, me), device_id_type=MESH)
-    pl.semaphore_signal(barrier, inc=1, device_id=(prv, me), device_id_type=MESH)
+    pl.semaphore_signal(barrier, inc=1, device_id=(nxt, dev(0, swap(nxt), 0)), device_id_type=MESH)
+    pl.semaphore_signal(barrier, inc=1, device_id=(prv, shard(0, 0, 0)), device_id_type=MESH)
 
     wide = jnp.broadcast_to(vir[...][None, :], (n_vir, n_vir))
     vsum[...] = wide + wide.T
@@ -60,7 +74,6 @@
         for n in lanes:
             at = k * n_vir + n * 128
             jcut[:, at:at + 128] = rows_in[n, pl.ds(picked + k, depth, stride=n_occ), :]
-    pl.semaphore_wait(barrier, 17)
 
     piece = depth // PIECES
 
@@ -70,33 +83,53 @@
             src_ref=jblock.at[at, :] if src is None else src, dst_ref=jblock.at[at, :],
             send_sem=jsend.at[n], recv_sem=jrecv.at[p, a], device_id=target, device_id_type=MESH)
 
-    hops = [jcopy(p, p, me, (nxt, me), jcut.at[p * piece:(p + 1) * piece, :]) for p in range(PIECES)]
+    def part(a, h):
+        size = depth // PARTS
+        return rows(a) if h is None else pl.ds(pl.multiple_of(a * depth + h * size, 8), size)
+
+    def xcopy(k, n, a, target, h=None):
+        return pltpu.make_async_remote_copy(
+            src_ref=staged.at[k, part(target, h), :], dst_ref=held.at[k, part(a, h), :],
+            send_sem=xsend.at[k, n], recv_sem=xrecv.at[k, a], device_id=(grp, target), device_id_type=MESH)
+
+    def ocopy(k, n, a, target, h=None):
+        return pltpu.make_async_remote_copy(
+            src_ref=dens.at[k, part(target, h), :], dst_ref=back.at[k, part(a, h), :],
+            send_sem=osend.at[k, n], recv_sem=orecv.at[k, a], device_id=(grp, target), device_id_type=MESH)
+
+    def stage(k, a):
+        for n in lanes:
+            staged[k, rows(a), n * 128:(n + 1) * 128] = rows_in[n, pl.ds(a * occ_block + k, depth, stride=n_occ), :]
+
+    first = [(0, n, h) for h in range(PARTS) for n in EARLY]
+    xorder = first + [e for e in [(k, n, h) for k in range(occ_block) for h in range(PARTS) for n in range(15)]
+                      if e not in first]
+    blocks = [(0, n) for n in EARLY] + [(0, n) for n in range(15) if n not in EARLY] + [(1, n) for n in range(15)]
+    done = [0]
+    ready = [0]
+
+    def xstage(count):
+        for k, n in blocks[ready[0]:ready[0] + count]:
+            stage(k, dev(*ROUTE[n]))
+        ready[0] += count
+
+    def xsend_some(count):
+        for k, n, h in xorder[done[0]:done[0] + count]:
+            xcopy(k, n, me, dev(*ROUTE[n]), h).start()
+        done[0] += count
+
+    xstage(FIRST)
+    pl.semaphore_wait(barrier, 17)
+    hops = [jcopy(p, p, me, (nxt, dev(0, swap(nxt), 0)), jcut.at[p * piece:(p + 1) * piece, :]) for p in range(PIECES)]
     for hop in hops:
         hop.start()
 
-    def xcopy(k, n, a, target):
-        return pltpu.make_async_remote_copy(
-            src_ref=staged.at[k, rows(target), :], dst_ref=held.at[k, rows(a), :],
-            send_sem=xsend.at[k, n], recv_sem=xrecv.at[k, a], device_id=(grp, target), device_id_type=MESH)
-
-    def ocopy(k, n, a, target):
-        return pltpu.make_async_remote_copy(
-            src_ref=dens.at[k, rows(target), :], dst_ref=back.at[k, rows(a), :],
-            send_sem=osend.at[k, n], recv_sem=orecv.at[k, a], device_id=(grp, target), device_id_type=MESH)
-
-    xorder = [(k, n) for k in range(occ_block) for n in range(len(ROUTE))]
-
-    def xsend_some(first, last):
-        for k, n in xorder[first:last]:
-            xcopy(k, n, me, dev(*ROUTE[n])).start()
-
     up, down, over, twin = dev(1, 0, 0), dev(3, 0, 0), dev(0, 1, 0), dev(0, 0, 1)
-    across, beyond, far = dev(1, 1, 0), dev(2, 0, 0), dev(2, 1, 0)
-    behind = dev(3, 1, 0)
-    by_y = ((me, (up, down, over)), (over, (up, down)), (down, (up,)), (across, (down,)),
-            (up, ()), (behind, ()), (beyond, ()), (far, ()))
-    by_z = ((me, (up, down, over)), (down, (over, up)), (up, (over,)), (across, (down,)),
-            (over, ()), (behind, ()), (beyond, ()), (far, ()))
+    own = (shard(0, 0, 0), (up, down, over))
+    opposite, above, below, across = shard(0, 1, 0), shard(1, 0, 0), shard(3, 0, 0), shard(1, 1, 0)
+    rest = ((shard(3, 1, 0), ()), (shard(2, 0, 0), ()), (shard(2, 1, 0), ()))
+    by_y = (own, (opposite, (up, down)), (below, (up,)), (across, (down,)), (above, ())) + rest
+    by_z = (own, (below, (over, up)), (above, (over,)), (across, (down,)), (opposite, ())) + rest
     plans = (by_z, by_y, by_z)
     sent = []
 
@@ -108,17 +141,19 @@
             copy.start()
             sent.append(copy)
 
-    for p, event in ((0, 0), (1, 0), (0, 1), (0, 2), (2, 0), (1, 1), (1, 2), (0, 3), (2, 1), (2, 2), (1, 3), (2, 3)):
+    xsend_some(FILL[0])
+    xstage(STAGE[0])
+    for at, (p, event) in enumerate(EVENTS):
         jrelay(p, event)
-    for d in range(n_aux):
-        for k in range(occ_block):
-            for n in lanes:
-                staged[k, d * depth:(d + 1) * depth, n * 128:(n + 1) * 128] = rows_in[
-                    n, pl.ds(d * occ_block + k, depth, stride=n_occ), :]
+        xsend_some(FILL[at + 1])
+        xstage(STAGE[at + 1])
+    xsend_some(15 * PARTS - done[0])
+    xstage(30 - ready[0])
+    xsend_some(30 * PARTS - done[0])
     for k in range(occ_block):
-        held[k, rows(me), :] = staged[k, rows(me), :]
-
-    xsend_some(0, 30)
+        for n in lanes:
+            held[k, rows(me), n * 128:(n + 1) * 128] = rows_in[
+                n, pl.ds(me * occ_block + k, depth, stride=n_occ), :]
     for event in range(4, 8):
         for p in range(PIECES):
             jrelay(p, event)
@@ -191,8 +226,9 @@
 
         lax.fori_loop(0, 4, second, 0)
         back[k, rows(me), :] = dens[k, rows(me), :]
-        for n, step in enumerate(ROUTE):
-            ocopy(k, n, me, dev(*step)).start()
+        for h in range(PARTS):
+            for n, step in enumerate(ROUTE):
+                ocopy(k, n, me, dev(*step), h).start()
         return 0
 
     lax.fori_loop(0, occ_block, half, 0)

time: 149 us -> 139 us (0.933)
  the two profiles are of different devices: /device:TPU:105 before, /device:TPU:49 now
where the time goes in v4:
time: 139 us; the launch traced here: 136 us
  Pallas kernels  136 us (98%)
    pallas_call x1, Pallas kernels, body(): pl.pallas_call(lambda *refs: kernel(sizes, *refs), out_shape=pltpu.VMEM((...  134 us

profile of v4, /device:TPU:49, one launch (start us, length us, event | category | flops | bytes accessed | tf_op | source)
XLA Modules:
  0.0 136.3 jit_solution(11262557329396011559)
XLA Ops:
  0.0 133.9 %shard_map.55.refs_0_ = f32[3,3072,128]{2,1,0:T(8,128)S(1)} custom-call(f32[256]{0:T(256)} %refs_0_.1, s32[256]{0:T(256)} %refs_1_.1, s32[1,8]{1,0:T(1,128)} %refs_2_.1, f32[384]{0:T(512)} %refs_3_.1, f32[3072,384]{1,0:T(8,128)} %bitcast.2), custom_call_target="tpu_custom_call" | custom-call | tf_op jit(solution)/shard_map/pallas_call | solution.py:277
  133.9 2.3 %shard_map.56 = f32[3072,384]{1,0:T(8,128)} custom-call(f32[3,3072,128]{2,1,0:T(8,128)S(1)} %shard_map.55.refs_0_), custom_call_target="tpu_custom_call" | custom-call | tf_op jit(solution)/shard_map/pallas_call | solution.py:312

commit v5 on v4

--- a/solution.py
+++ b/solution.py
@@ -8,15 +8,15 @@
 level_shift = 0.5
 MESH = pl.DeviceIdType.MESH
 
-PIECES = 3
-
-EVENTS = ((0, 0), (1, 0), (0, 1), (0, 2), (2, 0), (1, 1), (1, 2), (0, 3), (2, 1), (2, 2), (1, 3), (2, 3))
+PIECES = 6
+
+EVENTS = ((0, 0), (1, 0), (2, 0), (0, 1), (0, 2), (3, 0), (1, 1), (1, 2), (4, 0), (2, 1), (2, 2), (0, 3), (5, 0), (3, 1), (3, 2), (1, 3), (4, 1), (4, 2), (2, 3), (5, 1), (5, 2), (3, 3), (4, 3), (5, 3))
 EARLY = (0, 6, 3)
-FILL = (6, 0, 0, 0, 0, 0, 0, 0, 0, 0, 6, 0, 0)
+FILL = (9, 0, 0, 0, 0, 0, 0, 0, 0, 0, 0, 0, 0, 0, 0, 0, 0, 0, 0, 0, 0, 9, 0, 0, 0)
 FIRST = 3
-STAGE = (0, 0, 0, 0, 0, 12, 0, 0, 0, 0, 0, 0, 0)
-
-PARTS = 2
+STAGE = (0, 0, 0, 0, 0, 0, 0, 0, 0, 0, 12, 0, 0, 0, 0, 0, 0, 0, 0, 0, 0, 0, 0, 0, 0)
+
+PARTS = 3
 
 ROUTE = (
     (1, 0, 0), (3, 1, 0), (2, 1, 0), (0, 1, 0), (2, 0, 0),
@@ -130,7 +130,7 @@
     rest = ((shard(3, 1, 0), ()), (shard(2, 0, 0), ()), (shard(2, 1, 0), ()))
     by_y = (own, (opposite, (up, down)), (below, (up,)), (across, (down,)), (above, ())) + rest
     by_z = (own, (below, (over, up)), (above, (over,)), (across, (down,)), (opposite, ())) + rest
-    plans = (by_z, by_y, by_z)
+    plans = (by_z, by_y, by_z) * 2
     sent = []
 
     def jrelay(p, event):
@@ -234,13 +234,12 @@
     lax.fori_loop(0, occ_block, half, 0)
 
     for k in range(occ_block):
-        for a in range(n_aux):
-            @pl.when(a != me)
-            def _():
+        for dy, dz, dc in ((0, 0, 0),) + ROUTE:
+            a = dev(4 - dy, dz, dc)
+            if (dy, dz, dc) != (0, 0, 0):
                 ocopy(k, 0, a, twin).wait_recv()
             for n in lanes:
-                out[n, pl.ds(a * occ_block + k, depth, stride=n_occ), :] = back[
-                    k, a * depth:(a + 1) * depth, n * 128:(n + 1) * 128]
+                out[n, pl.ds(a * occ_block + k, depth, stride=n_occ), :] = back[k, rows(a), n * 128:(n + 1) * 128]
 
     for copy in hops + sent:
         copy.wait_send()

time: 139 us -> 135 us (0.971)
  Pallas kernels: 136 us -> 133 us
    pallas_call x1, Pallas kernels: 134 us -> 130 us  [body(): pl.pallas_call(lambda *refs: kernel(sizes, *refs), out_shape=pltpu.VMEM((...]
where the time goes in v5:
time: 135 us; the launch traced here: 133 us
  Pallas kernels  133 us (99%)
    pallas_call x1, Pallas kernels, body(): pl.pallas_call(lambda *refs: kernel(sizes, *refs), out_shape=pltpu.VMEM((...  130 us

profile of v5, /device:TPU:49, one launch (start us, length us, event | category | flops | bytes accessed | tf_op | source)
XLA Modules:
  0.0 132.8 jit_solution(9005045505899720673)
XLA Ops:
  0.0 130.3 %shard_map.55.refs_0_ = f32[3,3072,128]{2,1,0:T(8,128)S(1)} custom-call(f32[256]{0:T(256)} %refs_0_.1, s32[256]{0:T(256)} %refs_1_.1, s32[1,8]{1,0:T(1,128)} %refs_2_.1, f32[384]{0:T(512)} %refs_3_.1, f32[3072,384]{1,0:T(8,128)} %bitcast.2), custom_call_target="tpu_custom_call" | custom-call | tf_op jit(solution)/shard_map/pallas_call | solution.py:276
  130.3 2.3 %shard_map.56 = f32[3072,384]{1,0:T(8,128)} custom-call(f32[3,3072,128]{2,1,0:T(8,128)S(1)} %shard_map.55.refs_0_), custom_call_target="tpu_custom_call" | custom-call | tf_op jit(solution)/shard_map/pallas_call | solution.py:311

commit v6 on v5

--- a/solution.py
+++ b/solution.py
@@ -11,10 +11,14 @@
 PIECES = 6
 
 EVENTS = ((0, 0), (1, 0), (2, 0), (0, 1), (0, 2), (3, 0), (1, 1), (1, 2), (4, 0), (2, 1), (2, 2), (0, 3), (5, 0), (3, 1), (3, 2), (1, 3), (4, 1), (4, 2), (2, 3), (5, 1), (5, 2), (3, 3), (4, 3), (5, 3))
+AHEAD = 6
+AHEAD_STAGE = 10
+AHEAD_SEND = 21
+
 EARLY = (0, 6, 3)
-FILL = (9, 0, 0, 0, 0, 0, 0, 0, 0, 0, 0, 0, 0, 0, 0, 0, 0, 0, 0, 0, 0, 9, 0, 0, 0)
+FILL = (9, 0, 0, 0, 0, 0, 0, 0, 0, 0, 0, 0, 0, 0, 0, 0, 0, 0, 0, 0, 0, 3, 0, 0, 0)
 FIRST = 3
-STAGE = (0, 0, 0, 0, 0, 0, 0, 0, 0, 0, 12, 0, 0, 0, 0, 0, 0, 0, 0, 0, 0, 0, 0, 0, 0)
+STAGE = (0, 0, 0, 0, 0, 0, 0, 0, 0, 0, 6, 0, 0, 0, 0, 0, 0, 0, 0, 0, 0, 0, 0, 0, 0)
 
 PARTS = 3
 
@@ -108,14 +112,20 @@
     done = [0]
     ready = [0]
 
+    def stage_all(chosen):
+        for k, n in chosen:
+            stage(k, dev(*ROUTE[n]))
+
+    def send_all(chosen):
+        for k, n, h in chosen:
+            xcopy(k, n, me, dev(*ROUTE[n]), h).start()
+
     def xstage(count):
-        for k, n in blocks[ready[0]:ready[0] + count]:
-            stage(k, dev(*ROUTE[n]))
+        stage_all(blocks[ready[0]:ready[0] + count])
         ready[0] += count
 
     def xsend_some(count):
-        for k, n, h in xorder[done[0]:done[0] + count]:
-            xcopy(k, n, me, dev(*ROUTE[n]), h).start()
+        send_all(xorder[done[0]:done[0] + count])
         done[0] += count
 
     xstage(FIRST)
@@ -143,8 +153,21 @@
 
     xsend_some(FILL[0])
     xstage(STAGE[0])
+    later = (blocks[ready[0]:ready[0] + AHEAD], xorder[done[0]:done[0] + AHEAD])
+    ready[0] += AHEAD
+    done[0] += AHEAD
+
+    @pl.when(grp == 0)
+    def _():
+        stage_all(later[0])
+        send_all(later[1])
+
     for at, (p, event) in enumerate(EVENTS):
         jrelay(p, event)
+        if at + 1 == AHEAD_STAGE:
+            pl.when(grp != 0)(lambda: stage_all(later[0]))
+        if at + 1 == AHEAD_SEND:
+            pl.when(grp != 0)(lambda: send_all(later[1]))
         xsend_some(FILL[at + 1])
         xstage(STAGE[at + 1])
     xsend_some(15 * PARTS - done[0])
@@ -233,6 +256,12 @@
 
     lax.fori_loop(0, occ_block, half, 0)
 
+    for copy in hops + sent:
+        copy.wait_send()
+    for k in range(occ_block):
+        for n, step in enumerate(ROUTE):
+            xcopy(k, n, me, dev(*step)).wait_send()
+
     for k in range(occ_block):
         for dy, dz, dc in ((0, 0, 0),) + ROUTE:
             a = dev(4 - dy, dz, dc)
@@ -241,11 +270,8 @@
             for n in lanes:
                 out[n, pl.ds(a * occ_block + k, depth, stride=n_occ), :] = back[k, rows(a), n * 128:(n + 1) * 128]
 
-    for copy in hops + sent:
-        copy.wait_send()
     for k in range(occ_block):
         for n, step in enumerate(ROUTE):
-            xcopy(k, n, me, dev(*step)).wait_send()
             ocopy(k, n, me, dev(*step)).wait_send()
 
 

time: 135 us -> 135 us (level)
  no operation moved by 1% of the time
where the time goes in v6:
time: 135 us; the launch traced here: 133 us
  Pallas kernels  132 us (98%)
    pallas_call x1, Pallas kernels, body(): pl.pallas_call(lambda *refs: kernel(sizes, *refs), out_shape=pltpu.VMEM((...  130 us

profile of v6, /device:TPU:49, one launch (start us, length us, event | category | flops | bytes accessed | tf_op | source)
XLA Modules:
  0.0 132.5 jit_solution(17003893647561260902)
XLA Ops:
  0.0 130.1 %shard_map.55.refs_0_ = f32[3,3072,128]{2,1,0:T(8,128)S(1)} custom-call(f32[256]{0:T(256)} %refs_0_.1, s32[256]{0:T(256)} %refs_1_.1, s32[1,8]{1,0:T(1,128)} %refs_2_.1, f32[384]{0:T(512)} %refs_3_.1, f32[3072,384]{1,0:T(8,128)} %bitcast.2), custom_call_target="tpu_custom_call" | custom-call | tf_op jit(solution)/shard_map/pallas_call | solution.py:302
  130.1 2.3 %shard_map.56 = f32[3072,384]{1,0:T(8,128)} custom-call(f32[3,3072,128]{2,1,0:T(8,128)S(1)} %shard_map.55.refs_0_), custom_call_target="tpu_custom_call" | custom-call | tf_op jit(solution)/shard_map/pallas_call | solution.py:337

commit v7 on v6

--- a/solution.py
+++ b/solution.py
@@ -21,6 +21,8 @@
 STAGE = (0, 0, 0, 0, 0, 0, 0, 0, 0, 0, 6, 0, 0, 0, 0, 0, 0, 0, 0, 0, 0, 0, 0, 0, 0)
 
 PARTS = 3
+
+OUT_PARTS = 2
 
 ROUTE = (
     (1, 0, 0), (3, 1, 0), (2, 1, 0), (0, 1, 0), (2, 0, 0),
@@ -87,8 +89,8 @@
             src_ref=jblock.at[at, :] if src is None else src, dst_ref=jblock.at[at, :],
             send_sem=jsend.at[n], recv_sem=jrecv.at[p, a], device_id=target, device_id_type=MESH)
 
-    def part(a, h):
-        size = depth // PARTS
+    def part(a, h, parts=PARTS):
+        size = depth // parts
         return rows(a) if h is None else pl.ds(pl.multiple_of(a * depth + h * size, 8), size)
 
     def xcopy(k, n, a, target, h=None):
@@ -98,7 +100,7 @@
 
     def ocopy(k, n, a, target, h=None):
         return pltpu.make_async_remote_copy(
-            src_ref=dens.at[k, part(target, h), :], dst_ref=back.at[k, part(a, h), :],
+            src_ref=dens.at[k, part(target, h, OUT_PARTS), :], dst_ref=back.at[k, part(a, h, OUT_PARTS), :],
             send_sem=osend.at[k, n], recv_sem=orecv.at[k, a], device_id=(grp, target), device_id_type=MESH)
 
     def stage(k, a):
@@ -249,7 +251,7 @@
 
         lax.fori_loop(0, 4, second, 0)
         back[k, rows(me), :] = dens[k, rows(me), :]
-        for h in range(PARTS):
+        for h in range(OUT_PARTS):
             for n, step in enumerate(ROUTE):
                 ocopy(k, n, me, dev(*step), h).start()
         return 0

time: 135 us -> 134 us (level)
  no operation moved by 1% of the time
where the time goes in v7:
time: 134 us; the launch traced here: 132 us
  Pallas kernels  132 us (99%)
    pallas_call x1, Pallas kernels, body(): pl.pallas_call(lambda *refs: kernel(sizes, *refs), out_shape=pltpu.VMEM((...  129 us

profile of v7, /device:TPU:49, one launch (start us, length us, event | category | flops | bytes accessed | tf_op | source)
XLA Modules:
  0.0 131.9 jit_solution(10760886596432755649)
XLA Ops:
  0.0 129.5 %shard_map.55.refs_0_ = f32[3,3072,128]{2,1,0:T(8,128)S(1)} custom-call(f32[256]{0:T(256)} %refs_0_.1, s32[256]{0:T(256)} %refs_1_.1, s32[1,8]{1,0:T(1,128)} %refs_2_.1, f32[384]{0:T(512)} %refs_3_.1, f32[3072,384]{1,0:T(8,128)} %bitcast.2), custom_call_target="tpu_custom_call" | custom-call | tf_op jit(solution)/shard_map/pallas_call | solution.py:304
  129.5 2.3 %shard_map.56 = f32[3072,384]{1,0:T(8,128)} custom-call(f32[3,3072,128]{2,1,0:T(8,128)S(1)} %shard_map.55.refs_0_), custom_call_target="tpu_custom_call" | custom-call | tf_op jit(solution)/shard_map/pallas_call | solution.py:339
